TPU v7x, 32 devices: a whole 2x2x4 slice. The times are simulated.
32 devices in a mesh: groups: 2 (over y), ep: 4 (over z), half: 2 (over x), tp: 2 (over core).
Axes of the slice: x: 2, y: 2, z: 4, core: 2. Of those that a mesh axis runs over, the one named last changes fastest.
Arguments:
- queries: bfloat16 [512, 2048], P(('groups', 'ep', 'half'), 'tp'), parts along dimension 0, may hold values from -6 to 6
- new_keys: bfloat16 [512, 256], P(('groups', 'ep', 'half'), 'tp'), parts along dimension 0, may hold values from -4 to 4
- new_values: bfloat16 [512, 256], P(('groups', 'ep', 'half'), 'tp'), parts along dimension 0, may hold values from -4 to 4
- cache_keys: bfloat16 [512, 2, 64, 128], P(('groups', 'ep', 'half'), 'tp'), parts along dimension 0, may hold values from -4 to 4
- cache_values: bfloat16 [512, 2, 64, 128], P(('groups', 'ep', 'half'), 'tp'), parts along dimension 0, may hold values from -4 to 4
- lengths: int32 [512], P(('groups', 'ep', 'half')), parts along dimension 0, may hold values from 1 to 64, as said below
- out_weight: bfloat16 [2048, 2048], P('tp', 'half'), may hold values from -0.375 to 0.375
- residual: bfloat16 [512, 2048], P(('groups', 'ep'), 'half'), parts along dimension 0, may hold values from -5 to 5
- norm_gain: float32 [2048], P('half'), may hold values from 0.1 to 1.9
- expert_ids: int32 [512, 8], P(('groups', 'ep')), parts along dimension 0, may hold values from 0 to 63, all different within a row; in each aligned block of 64 rows (0 to 63, 64 to 127, ...) at most 12 rows name the same one
- gate_weights: float32 [512, 8], P(('groups', 'ep')), parts along dimension 0, may hold values from 0.05 to 1
- w_gate: bfloat16 [64, 768, 2048], P(('ep', 'tp'), 'half'), may hold values from -0.125 to 0.125
- w_up: bfloat16 [64, 768, 2048], P(('ep', 'tp'), 'half'), may hold values from -0.125 to 0.125
- w_down: bfloat16 [64, 768, 2048], P(('ep', 'tp'), 'half'), may hold values from -0.625 to 0.625
Outputs:
- layer_out: bfloat16 [512, 2048], P(('groups', 'ep'), ('half', 'tp')), parts along dimension 0
There are 2 independent parts, one for each index of `groups`. A program takes and returns all parts, laid end to end along the dimension named above; an argument that names none is the same for every part. Nothing has to cross between parts.
Inputs may be any that keep to these rules, and one draw needn't show every extreme that they name: `expert_ids`: in each block of 64 consecutive rows (the tokens of one index of ep) no expert is named by more than 12 rows. `lengths`: among each device's 32 requests one has 64 cached tokens.
All inputs are finite; a program needn't handle non-finite values.
Results may differ from a plain program's by a relative error of at most 0.014.
Values may be sent and summed in bfloat16 or wider, within the bound.
No kernel may reach another device: no remote copies, remote signals or barrier semaphores. Data moves between devices by JAX's collectives and lax.ppermute only.
A program may use at most 128 MiB of HBM per device.

v0:
```python
import math
import jax
import jax.numpy as jnp
from jax import lax
from jax.sharding import PartitionSpec as P

EXPERTS = 64
EPSILON = 1e-06


def attend(queries, new_keys, new_values, cache_keys, cache_values, lengths):
    requests, key_heads, context, head_size = cache_keys.shape
    sharing = queries.shape[1] // (key_heads * head_size)
    query_blocks = queries.reshape(requests, key_heads, sharing, head_size)
    score_scale = 1.0 / math.sqrt(head_size)
    scores = (
        jnp.einsum("rkgd,rkcd->rkgc", query_blocks, cache_keys, preferred_element_type=jnp.float32)
        * score_scale
    )
    own_score = (
        jnp.einsum(
            "rkgd,rkd->rkg",
            query_blocks,
            new_keys.reshape(requests, key_heads, head_size),
            preferred_element_type=jnp.float32,
        )
        * score_scale
    )
    valid = lax.iota(jnp.int32, context)[None, :] < lengths[:, None]
    scores = jnp.where(valid[:, None, None, :], scores, -1e30)
    highest = jnp.maximum(jnp.max(scores, axis=-1), own_score)
    weights = jnp.exp(scores - highest[..., None])
    own_weight = jnp.exp(own_score - highest)
    denominator = jnp.sum(weights, axis=-1) + own_weight
    probs = (weights / denominator[..., None]).astype(jnp.bfloat16)
    own_prob = (own_weight / denominator).astype(jnp.bfloat16)
    mixture = jnp.einsum("rkgc,rkcd->rkgd", probs, cache_values, preferred_element_type=jnp.float32)
    mixture = mixture + own_prob.astype(jnp.float32)[..., None] * new_values.reshape(
        requests, key_heads, 1, head_size
    ).astype(jnp.float32)
    return mixture.astype(jnp.bfloat16).reshape(requests, key_heads * sharing * head_size)


def combine_rows(returned_rows, target, gates):
    token_rows, top_count = target.shape
    safe_target = jnp.maximum(target, 0).reshape(-1)
    picked = jnp.take(returned_rows, safe_target, axis=0).reshape(
        token_rows, top_count, returned_rows.shape[1]
    )
    weighting = jnp.where(target >= 0, gates, 0.0)
    return jnp.sum(picked.astype(jnp.float32) * weighting[..., None], axis=1)


def on_device(
    queries,
    new_keys,
    new_values,
    cache_keys,
    cache_values,
    lengths,
    out_weight,
    residual,
    norm_gain,
    expert_ids,
    gate_weights,
    w_gate,
    w_up,
    w_down,
):
    attended = attend(queries, new_keys, new_values, cache_keys, cache_values, lengths)
    partial_mix = jnp.dot(
        lax.all_gather(attended, "half", axis=0, tiled=True),
        out_weight,
        preferred_element_type=jnp.float32,
    )
    mixed = lax.psum(partial_mix.astype(jnp.bfloat16), "tp").astype(jnp.float32)
    hidden = residual.astype(jnp.float32) + mixed
    squares = lax.psum(jnp.sum(hidden * hidden, axis=1), "half")
    half_width = hidden.shape[1]
    width = half_width * lax.axis_size("half")
    normed = (hidden * lax.rsqrt(squares / width + EPSILON)[:, None] * norm_gain[None, :]).astype(
        jnp.bfloat16
    )
    token_rows, top_count = expert_ids.shape
    ep_count = lax.axis_size("ep")
    tp_count = lax.axis_size("tp")
    local_experts = w_gate.shape[0]
    capacity = token_rows * top_count * 3 // (2 * EXPERTS)
    slot_count = ep_count * local_experts * capacity
    flat_ids = expert_ids.reshape(-1)
    one_hot = (flat_ids[:, None] == lax.iota(jnp.int32, EXPERTS)[None, :]).astype(jnp.int32)
    earlier = jnp.cumsum(one_hot, axis=0) - one_hot
    slot = jnp.sum(earlier * one_hot, axis=1)
    owner_ep = flat_ids // (local_experts * tp_count)
    owner_tp = flat_ids // local_experts % tp_count
    target = owner_ep * (local_experts * capacity) + flat_ids % local_experts * capacity + slot
    target = jnp.where(owner_tp == lax.axis_index("tp"), target, -1).reshape(token_rows, top_count)
    dispatch_matrix = jnp.any(
        lax.iota(jnp.int32, slot_count)[:, None, None] == target[None, :, :], axis=2
    ).astype(jnp.bfloat16)
    gates = gate_weights / jnp.sum(gate_weights, axis=1, keepdims=True)
    full_rows = lax.all_gather(normed, "half", axis=1, tiled=True)
    outgoing = jnp.dot(dispatch_matrix, full_rows, preferred_element_type=jnp.float32).astype(
        jnp.bfloat16
    )
    arrived = lax.all_to_all(
        outgoing.reshape(ep_count, local_experts, capacity, width),
        "ep",
        split_axis=0,
        concat_axis=0,
        tiled=True,
    )
    gate_part = jnp.einsum("secd,efd->secf", arrived, w_gate, preferred_element_type=jnp.float32)
    up_part = jnp.einsum("secd,efd->secf", arrived, w_up, preferred_element_type=jnp.float32)
    activation = (jax.nn.silu(gate_part) * up_part).astype(jnp.bfloat16)
    expert_out = jnp.einsum(
        "secf,efd->secd", activation, w_down, preferred_element_type=jnp.float32
    ).astype(jnp.bfloat16)
    summed = lax.psum_scatter(
        expert_out.astype(jnp.float32).astype(jnp.bfloat16), "half", scatter_dimension=3, tiled=True
    ).astype(jnp.float32)
    returned = lax.all_to_all(
        summed.reshape(ep_count, local_experts * capacity, half_width).astype(jnp.bfloat16),
        "ep",
        split_axis=0,
        concat_axis=0,
        tiled=True,
    ).astype(jnp.float32)
    term = combine_rows(returned.reshape(slot_count, half_width), target, gates)
    expert_sum = lax.psum_scatter(
        term.astype(jnp.bfloat16), "tp", scatter_dimension=1, tiled=True
    ).astype(jnp.float32)
    slice_width = expert_sum.shape[1]
    own_columns = lax.dynamic_slice_in_dim(
        hidden, lax.axis_index("tp") * slice_width, slice_width, 1
    )
    return (own_columns + expert_sum).astype(jnp.bfloat16)


def solution(mesh):
    placed = (
        P(("groups", "ep", "half"), "tp"),
        P(("groups", "ep", "half"), "tp"),
        P(("groups", "ep", "half"), "tp"),
        P(("groups", "ep", "half"), "tp", None, None),
        P(("groups", "ep", "half"), "tp", None, None),
        P(("groups", "ep", "half")),
        P("tp", "half"),
        P(("groups", "ep"), "half"),
        P("half"),
        P(("groups", "ep"), None),
        P(("groups", "ep"), None),
        P(("ep", "tp"), "half", None),
        P(("ep", "tp"), "half", None),
        P(("ep", "tp"), "half", None),
    )
    return jax.shard_map(
        on_device,
        mesh=mesh,
        in_specs=placed,
        out_specs=P(("groups", "ep"), ("half", "tp")),
        check_vma=False,
    )
```

profile of v0, /device:TPU:0, one launch (start us, length us, event | category | flops | bytes accessed | tf_op | source)
XLA Modules:
  0.0 210.5 jit_solution(17106588360139845303)
XLA Ops:
  6.5 1.0 copy.78
  7.5 0.7 iota_compare_fusion.3
  8.3 0.8 fusion.58
  9.1 1.5 fusion.76
  10.6 0.2 fusion.55
  10.9 0.7 convert_element_type.73
  11.6 1.4 fusion.41
  13.0 6.0 %all_gather.6 = bf16[64,1024]{1,0:T(8,128)(2,1)S(1)} all-gather(bf16[32,1024]{1,0:T(8,128)(2,1)S(1)} %bitcast.97), channel_id=1, replica_groups=mesh['groups'=2,'ep'=4,'half'=2,'tp'=2] {'half'}, dimensions={0}, use_global_device_ids=true | all-gather | bytes 196608 | tf_op jit(solution)/shard_map/all_gather | solution.py:72
  19.0 1.1 convolution_convert_fusion.1
  20.1 0.0 reduce-scatter.3.cloned.1.call-start
  20.2 0.1 copy.59
  20.3 0.1 eq.56
  20.4 0.1 eq.52
  20.5 1.2 reduce-window.6
  21.7 0.2 slice_reduce_fusion
  22.0 0.1 fusion.53
  22.1 0.1 reduce_sum.49
  22.2 0.1 copy.62
  22.3 0.1 copy.64
  22.4 0.3 fusion.47
  22.7 17.3 %all-reduce.2.cloned.1.call-done = bf16[64,1024]{1,0:T(8,128)(2,1)} async-done(((bf16[64,1024]{1,0:T(8,128)(2,1)}), bf16[64,1024]{1,0:T(8,128)(2,1)}) %all-reduce.2.cloned.1.call-update) | async-done | bytes 131088 | tf_op jit(solution)/shard_map/psum | solution.py:76
  40.0 1.0 convert_add_fusion
  41.0 4.9 %psum.15 = f32[64]{0:T(128)S(1)} all-reduce(f32[64]{0:T(128)S(1)} %get-tuple-element.8), channel_id=1, replica_groups=mesh['groups'=2,'ep'=4,'half'=2,'tp'=2] {'half'}, use_global_device_ids=true, to_apply=%region_8.9 | all-reduce | flops 64 | bytes 512 | tf_op jit(solution)/shard_map/psum | solution.py:78
  46.0 1.0 multiply_convert_fusion
  47.0 5.6 %all_gather.7 = bf16[64,2048]{1,0:T(8,128)(2,1)S(1)} all-gather(bf16[64,1024]{1,0:T(8,128)(2,1)S(1)} %multiply_convert_fusion), channel_id=1, replica_groups=mesh['groups'=2,'ep'=4,'half'=2,'tp'=2] {'half'}, dimensions={1}, use_global_device_ids=true | all-gather | bytes 393216 | tf_op jit(solution)/shard_map/all_gather | solution.py:102
  52.6 1.8 convolution_convert_fusion
  54.4 3.6 %reshape.224 = bf16[4,8,12,2048]{3,2,1,0:T(8,128)(2,1)} reshape(bf16[384,2048]{1,0:T(8,128)(2,1)} %convolution_convert_fusion) | data formatting | bytes 3145728 | tf_op jit(solution)/shard_map/reshape | solution.py:107
  58.0 2.5 %copy.65 = bf16[4,8,12,2048]{3,1,2,0:T(8,128)(2,1)S(1)} copy(bf16[4,8,12,2048]{3,2,1,0:T(8,128)(2,1)} %reshape.224) | data formatting | bytes 3145728 | tf_op jit(solution)/shard_map/reshape | solution.py:107
  60.5 39.8 %all_to_all.10 = bf16[4,8,12,2048]{3,1,2,0:T(8,128)(2,1)S(1)} all-to-all(bf16[4,8,12,2048]{3,1,2,0:T(8,128)(2,1)S(1)} %copy.65), channel_id=1, replica_groups=mesh['groups'=2,'ep'=4,'half'=2,'tp'=2] {'ep'}, dimensions={0} | all-to-all | bytes 3145728 | tf_op jit(solution)/shard_map/all_to_all | solution.py:106
  100.2 1.1 copy-done.1
  101.4 8.7 %fusion.16 = f32[4,8,12,384]{3,2,0,1:T(8,128)S(1)} fusion(bf16[8,384,2048]{2,1,0:T(8,128)(2,1)} %param.25, bf16[4,8,12,2048]{3,1,2,0:T(8,128)(2,1)S(1)} %all_to_all.10), kind=kOutput, calls=%fused_computation.15 | convolution fusion | flops 603979776 | bytes 14745600 | tf_op jit(solution)/shard_map/secd,efd->secf/dot_general | solution.py:113
  110.1 18.4 %fusion.9 = bf16[4,8,12,2048]{3,2,0,1:T(8,128)(2,1)} fusion(bf16[8,384,2048]{2,1,0:T(8,128)(2,1)} %param.27, bf16[8,384,2048]{2,1,0:T(8,128)(2,1)} %param.26, bf16[4,8,12,2048]{3,1,2,0:T(8,128)(2,1)} %copy-done.1, f32[4,8,12,384]{3,2,0,1:T(8,128)S(1)} %fusion.16), kind=kOutput, calls=%fused_computation.9 | convolution fusion | flops 1209630720 | bytes 28901376 | tf_op jit(solution)/shard_map/secf,efd->secd/dot_general | solution.py:116
  128.5 0.0 reduce-scatter.3.cloned.1.call-update
  128.5 31.1 %reduce-scatter.3.cloned.1.call-done = bf16[4,8,12,1024]{3,2,0,1:T(8,128)(2,1)} async-done(((bf16[4,8,12,2048]{3,2,0,1:T(8,128)(2,1)}), bf16[4,8,12,1024]{3,2,0,1:T(8,128)(2,1)}) %reduce-scatter.3.cloned.1.call-update) | async-done | bytes 786448 | tf_op jit(solution)/shard_map/reduce_scatter | solution.py:119
  159.6 1.8 copy.68
  161.4 1.1 copy.69
  162.5 4.6 %all-to-all-start.1 = ((bf16[4,96,1024]{2,1,0:T(8,128)(2,1)}), bf16[4,96,1024]{2,1,0:T(8,128)(2,1)S(1)}, u32[]{:S(2)}, u32[]{:S(2)}) async-start(bf16[4,96,1024]{2,1,0:T(8,128)(2,1)} %copy.69), calls=%async_computation.2 | async-start | bytes 1572864 | tf_op jit(solution)/shard_map/all_to_all | solution.py:122
  167.1 0.1 copy.70
  167.2 0.1 reshape.227
  167.3 0.1 copy.71
  167.4 0.1 copy.63
  167.6 19.5 %all-to-all-done.1 = bf16[4,96,1024]{2,1,0:T(8,128)(2,1)S(1)} async-done(((bf16[4,96,1024]{2,1,0:T(8,128)(2,1)}), bf16[4,96,1024]{2,1,0:T(8,128)(2,1)S(1)}, u32[]{:S(2)}, u32[]{:S(2)}) %all-to-all-start.1) | async-done | bytes 786464 | tf_op jit(solution)/shard_map/all_to_all | solution.py:122
  187.1 1.4 bitcast_convert_fusion
  188.5 5.1 %gather_fusion = f32[512,1024]{1,0:T(8,128)} fusion(f32[384,1024]{1,0:T(8,128)} %bitcast_convert_fusion, s32[1024]{0:T(1024)S(1)} %pad_clamp_fusion), kind=kCustom, calls=%fused_computation | custom fusion | bytes 4196352 | tf_op jit(solution)/shard_map/jit(_take)/gather | solution.py:47
  193.5 3.0 %fusion.15 = bf16[64,1024]{1,0:T(8,128)(2,1)} fusion(f32[512,1024]{1,0:T(8,128)} %gather_fusion, f32[64,8]{1,0:T(8,128)S(1)} %copy.71, pred[64,8]{1,0:T(8,128)(4,1)S(1)} %copy.63), kind=kLoop, calls=%fused_computation.14 | loop fusion | flops 1507328 | bytes 2230784 | tf_op jit(solution)/shard_map/reduce_sum | solution.py:51
  196.6 0.0 reduce-scatter.5.cloned.1.call-update
  196.6 5.9 %reduce-scatter.5.cloned.1.call-done = bf16[64,512]{1,0:T(8,128)(2,1)} async-done(((bf16[64,1024]{1,0:T(8,128)(2,1)}), bf16[64,512]{1,0:T(8,128)(2,1)}) %reduce-scatter.5.cloned.1.call-update) | async-done | bytes 65552 | tf_op jit(solution)/shard_map/reduce_scatter | solution.py:130
  202.5 1.5 add_convert_fusion
  (27 shorter events, 0.2 us)
Async XLA Ops:
  6.5 12.4 %copy-start = (bf16[1024,1024]{1,0:T(8,128)(2,1)S(1)}, bf16[1024,1024]{1,0:T(8,128)(2,1)}, u32[]{:S(2)}) copy-start(bf16[1024,1024]{1,0:T(8,128)(2,1)} %param.20) | copy-start | bytes 6291460
  6.5 33.5 %all-reduce.2.cloned.1.call-start = ((), (), s32[]{:S(2)}) async-start(), calls=%async_computation.4 | async-start | bytes 262144 | tf_op jit(solution)/shard_map/psum | solution.py:76
  10.6 9.5 %copy-start.3 = (s32[64,8]{0,1:T(8,128)S(1)}, s32[64,8]{0,1:T(8,128)}, u32[]{:S(2)}) copy-start(s32[64,8]{0,1:T(8,128)} %param.23) | copy-start | bytes 6148
  12.9 27.1 %copy-start.2 = (bf16[64,1024]{1,0:T(8,128)(2,1)S(1)}, bf16[64,1024]{1,0:T(8,128)(2,1)}, u32[]{:S(2)}) copy-start(bf16[64,1024]{1,0:T(8,128)(2,1)} %param.21) | copy-start | bytes 393220
  13.0 33.0 %copy-start.5 = (f32[1024]{0:T(1024)S(1)}, f32[1024]{0:T(1024)}, u32[]{:S(2)}) copy-start(f32[1024]{0:T(1024)} %param.22) | copy-start | bytes 12292
  20.1 139.5 %reduce-scatter.3.cloned.1.call-start = ((), (), s32[]{:S(2)}) async-start(), calls=%async_computation.5 | async-start | bytes 3145728 | tf_op jit(solution)/shard_map/reduce_scatter | solution.py:119
  100.2 1.1 copy-start.1
  128.5 38.8 %copy-start.4 = (f32[64,8]{0,1:T(8,128)S(1)}, f32[64,8]{0,1:T(8,128)}, u32[]{:S(2)}) copy-start(f32[64,8]{0,1:T(8,128)} %param.24) | copy-start | bytes 6148
  162.5 24.5 %all-to-all-start.1 = ((bf16[4,96,1024]{2,1,0:T(8,128)(2,1)}), bf16[4,96,1024]{2,1,0:T(8,128)(2,1)S(1)}, u32[]{:S(2)}, u32[]{:S(2)}) async-start(bf16[4,96,1024]{2,1,0:T(8,128)(2,1)} %copy.69), calls=%async_computation.2 | async-start | bytes 1572864 | tf_op jit(solution)/shard_map/all_to_all | solution.py:122
  167.1 35.3 %reduce-scatter.5.cloned.1.call-start = ((), (), s32[]{:S(2)}) async-start(), calls=%async_computation.6 | async-start | bytes 196608 | tf_op jit(solution)/shard_map/reduce_scatter | solution.py:130
Sparse Core Ops, SparseCore 0:
  20.2 19.6 all-reduce.1
  128.6 30.9 reduce-scatter.2
  196.7 5.7 reduce-scatter.4
where the time goes:
time: 211 us; the launch traced here: 210 us
  waiting for transfers between devices  73.9 us (35%)
  blocking collectives  56.3 us (27%)
  matrix products  33.7 us (16%)
  local copies, waits for them, and re-layouts  17.4 us (8%)
  between operations  13.3 us (6%)
  other arithmetic  11.3 us (5%)
  starting transfers between devices  4.62 us (2%)
    all_to_all x1, blocking collectives, on_device(): lax.all_to_all(outgoing.reshape(ep_count, local_experts, capacity, width)...  39.8 us
    reduce_scatter x1, waiting for transfers between devices, on_device(): lax.psum_scatter(expert_out.astype(jnp.float32).astype(jnp.bfloat16), 'ha...  31.1 us
    all_to_all x1, waiting for transfers between devices, on_device(): lax.all_to_all(summed.reshape(ep_count, local_experts * capacity, half_wi...  19.5 us
    dot_general x1, matrix products, on_device(): jnp.einsum('secf,efd->secd', activation, w_down, preferred_element_type=j...  18.4 us
    psum x1, waiting for transfers between devices, on_device(): mixed = lax.psum(partial_mix.astype(jnp.bfloat16), 'tp').astype(jnp.float32)  17.3 us
    dot_general x1, matrix products, on_device(): jnp.einsum('secd,efd->secf', arrived, w_gate, preferred_element_type=jnp....  8.68 us
    reshape x2, local copies, waits for them, and re-layouts, on_device(): outgoing.reshape(ep_count, local_experts, capacity, width)  6.06 us
    all_gather x1, blocking collectives, on_device(): lax.all_gather(attended, 'half', axis=0, tiled=True)  6 us
  transfers between devices with their start and end apart: 4, of which 4 were waited for; matrix products, arithmetic and copies ran while one was open for 1% of the time, Pallas kernels for 0%

commit v1 on v0

--- a/solution.py
+++ b/solution.py
@@ -6,6 +6,22 @@
 
 EXPERTS = 64
 EPSILON = 1e-06
+
+
+def swapped_with_each(value, axis, split, join):
+    ways, here = (lax.axis_size(axis), lax.axis_index(axis))
+    width = value.shape[split] // ways
+    lengths = list(value.shape)
+    lengths[split] = width
+    height = lengths[join]
+    lengths[join] = height * ways
+    full = jnp.zeros(lengths, value.dtype)
+    for mask in range(ways):
+        part = lax.dynamic_slice_in_dim(value, (here ^ mask) * width, width, axis=split)
+        if mask:
+            part = lax.ppermute(part, axis, [(d, d ^ mask) for d in range(ways)])
+        full = lax.dynamic_update_slice_in_dim(full, part, (here ^ mask) * height, axis=join)
+    return full
 
 
 def attend(queries, new_keys, new_values, cache_keys, cache_values, lengths):
@@ -119,12 +135,11 @@
     summed = lax.psum_scatter(
         expert_out.astype(jnp.float32).astype(jnp.bfloat16), "half", scatter_dimension=3, tiled=True
     ).astype(jnp.float32)
-    returned = lax.all_to_all(
+    returned = swapped_with_each(
         summed.reshape(ep_count, local_experts * capacity, half_width).astype(jnp.bfloat16),
         "ep",
-        split_axis=0,
-        concat_axis=0,
-        tiled=True,
+        0,
+        0,
     ).astype(jnp.float32)
     term = combine_rows(returned.reshape(slot_count, half_width), target, gates)
     expert_sum = lax.psum_scatter(

time: 211 us -> 225 us (1.066)
  waiting for transfers between devices: 73.9 us -> 86.8 us
    ppermute x0 -> x3, waiting for transfers between devices: none -> 26.6 us  [swapped_with_each(): part = lax.ppermute(part, axis, [(d, d ^ mask) for d in range(ways)])]
    all_to_all x1 -> x0, waiting for transfers between devices: 19.5 us -> none  [on_device(): lax.all_to_all(summed.reshape(ep_count, local_experts * capacity, half_wi...]
    reduce_scatter x1, waiting for transfers between devices: 5.87 us -> 12.7 us  [on_device(): lax.psum_scatter(term.astype(jnp.bfloat16), 'tp', scatter_dimension=1, ti...]
    all_to_all x1 -> x0, starting transfers between devices: 4.58 us -> none  [on_device(): lax.all_to_all(summed.reshape(ep_count, local_experts * capacity, half_wi...]
    ppermute x0 -> x3, starting transfers between devices: none -> 4.45 us  [swapped_with_each(): part = lax.ppermute(part, axis, [(d, d ^ mask) for d in range(ways)])]
  transfers between devices with their start and end apart: 4 -> 6, of which waited for: 4 -> 5; matrix products, arithmetic and copies ran while one was open for 1% -> 1% of each run, Pallas kernels for 0% -> 0%
where the time goes in v1:
time: 225 us
  waiting for transfers between devices  86.8 us (39%)
  blocking collectives  56.3 us (25%)
  matrix products  33.7 us (15%)
  local copies, waits for them, and re-layouts  18.4 us (8%)
  between operations  13.4 us (6%)
  other arithmetic  11.3 us (5%)
  starting transfers between devices  4.76 us (2%)
    all_to_all x1, blocking collectives, on_device(): lax.all_to_all(outgoing.reshape(ep_count, local_experts, capacity, width)...  39.8 us
    reduce_scatter x1, waiting for transfers between devices, on_device(): lax.psum_scatter(expert_out.astype(jnp.float32).astype(jnp.bfloat16), 'ha...  30.2 us
    ppermute x3, waiting for transfers between devices, swapped_with_each(): part = lax.ppermute(part, axis, [(d, d ^ mask) for d in range(ways)])  26.6 us
    dot_general x1, matrix products, on_device(): jnp.einsum('secf,efd->secd', activation, w_down, preferred_element_type=j...  18.4 us
    psum x1, waiting for transfers between devices, on_device(): mixed = lax.psum(partial_mix.astype(jnp.bfloat16), 'tp').astype(jnp.float32)  17.3 us
    reduce_scatter x1, waiting for transfers between devices, on_device(): lax.psum_scatter(term.astype(jnp.bfloat16), 'tp', scatter_dimension=1, ti...  12.7 us
    dot_general x1, matrix products, on_device(): jnp.einsum('secd,efd->secf', arrived, w_gate, preferred_element_type=jnp....  8.69 us
    reshape x2, local copies, waits for them, and re-layouts, on_device(): outgoing.reshape(ep_count, local_experts, capacity, width)  6.06 us
  transfers between devices with their start and end apart: 6, of which 5 were waited for; matrix products, arithmetic and copies ran while one was open for 1% of the time, Pallas kernels for 0%

profile of v1, /device:TPU:0, one launch (start us, length us, event | category | flops | bytes accessed | tf_op | source)
XLA Modules:
  0.0 224.7 jit_solution(9612071119026510143)
XLA Ops:
  6.5 1.0 copy.90
  7.5 0.7 iota_compare_fusion.3
  8.3 0.8 fusion.58
  9.1 1.5 fusion.76
  10.6 0.2 fusion.55
  10.9 0.7 convert_element_type.73
  11.6 1.4 fusion.41
  13.0 6.0 %all_gather.6 = bf16[64,1024]{1,0:T(8,128)(2,1)S(1)} all-gather(bf16[32,1024]{1,0:T(8,128)(2,1)S(1)} %bitcast.97), channel_id=1, replica_groups=mesh['groups'=2,'ep'=4,'half'=2,'tp'=2] {'half'}, dimensions={0}, use_global_device_ids=true | all-gather | bytes 196608 | tf_op jit(solution)/shard_map/all_gather | solution.py:88
  19.0 1.1 convolution_convert_fusion.1
  20.2 0.1 copy.68
  20.3 0.1 eq.56
  20.4 0.1 eq.52
  20.5 1.2 reduce-window.6
  21.7 0.2 slice_reduce_fusion
  22.0 0.1 fusion.53
  22.1 0.1 reduce_sum.49
  22.3 0.1 copy.73
  22.4 0.3 fusion.47
  22.7 17.3 %all-reduce.2.cloned.1.call-done = bf16[64,1024]{1,0:T(8,128)(2,1)} async-done(((bf16[64,1024]{1,0:T(8,128)(2,1)}), bf16[64,1024]{1,0:T(8,128)(2,1)}) %all-reduce.2.cloned.1.call-update) | async-done | bytes 131088 | tf_op jit(solution)/shard_map/psum | solution.py:92
  40.0 1.0 convert_add_fusion
  41.0 4.9 %psum.15 = f32[64]{0:T(128)S(1)} all-reduce(f32[64]{0:T(128)S(1)} %get-tuple-element.12), channel_id=1, replica_groups=mesh['groups'=2,'ep'=4,'half'=2,'tp'=2] {'half'}, use_global_device_ids=true, to_apply=%region_8.9 | all-reduce | flops 64 | bytes 512 | tf_op jit(solution)/shard_map/psum | solution.py:94
  46.0 1.0 multiply_convert_fusion
  47.0 5.6 %all_gather.7 = bf16[64,2048]{1,0:T(8,128)(2,1)S(1)} all-gather(bf16[64,1024]{1,0:T(8,128)(2,1)S(1)} %multiply_convert_fusion), channel_id=1, replica_groups=mesh['groups'=2,'ep'=4,'half'=2,'tp'=2] {'half'}, dimensions={1}, use_global_device_ids=true | all-gather | bytes 393216 | tf_op jit(solution)/shard_map/all_gather | solution.py:118
  52.6 1.8 convolution_convert_fusion
  54.4 3.6 %reshape.224 = bf16[4,8,12,2048]{3,2,1,0:T(8,128)(2,1)} reshape(bf16[384,2048]{1,0:T(8,128)(2,1)} %convolution_convert_fusion) | data formatting | bytes 3145728 | tf_op jit(solution)/shard_map/reshape | solution.py:123
  58.0 2.5 %copy.74 = bf16[4,8,12,2048]{3,1,2,0:T(8,128)(2,1)S(1)} copy(bf16[4,8,12,2048]{3,2,1,0:T(8,128)(2,1)} %reshape.224) | data formatting | bytes 3145728 | tf_op jit(solution)/shard_map/reshape | solution.py:123
  60.5 39.8 %all_to_all.5 = bf16[4,8,12,2048]{3,1,2,0:T(8,128)(2,1)S(1)} all-to-all(bf16[4,8,12,2048]{3,1,2,0:T(8,128)(2,1)S(1)} %copy.74), channel_id=1, replica_groups=mesh['groups'=2,'ep'=4,'half'=2,'tp'=2] {'ep'}, dimensions={0} | all-to-all | bytes 3145728 | tf_op jit(solution)/shard_map/all_to_all | solution.py:122
  100.2 1.1 copy-done.1
  101.4 8.7 %fusion.16 = f32[4,8,12,384]{3,2,0,1:T(8,128)S(1)} fusion(bf16[8,384,2048]{2,1,0:T(8,128)(2,1)} %param.25, bf16[4,8,12,2048]{3,1,2,0:T(8,128)(2,1)S(1)} %all_to_all.5), kind=kOutput, calls=%fused_computation.15 | convolution fusion | flops 603979776 | bytes 14745600 | tf_op jit(solution)/shard_map/secd,efd->secf/dot_general | solution.py:129
  110.1 18.4 %fusion.9 = bf16[4,8,12,2048]{3,2,0,1:T(8,128)(2,1)} fusion(bf16[8,384,2048]{2,1,0:T(8,128)(2,1)} %param.27, bf16[8,384,2048]{2,1,0:T(8,128)(2,1)} %param.26, bf16[4,8,12,2048]{3,1,2,0:T(8,128)(2,1)} %copy-done.1, f32[4,8,12,384]{3,2,0,1:T(8,128)S(1)} %fusion.16), kind=kOutput, calls=%fused_computation.9 | convolution fusion | flops 1209630720 | bytes 28901376 | tf_op jit(solution)/shard_map/secf,efd->secd/dot_general | solution.py:132
  128.5 0.3 reduce-scatter.5.cloned.1.call-start
  128.9 0.1 reshape.227
  129.0 0.2 copy-done.4
  129.2 0.1 copy.83
  129.3 0.1 copy.72
  129.4 30.2 %reduce-scatter.3.cloned.1.call-done = bf16[4,8,12,1024]{3,2,0,1:T(8,128)(2,1)} async-done(((bf16[4,8,12,2048]{3,2,0,1:T(8,128)(2,1)}), bf16[4,8,12,1024]{3,2,0,1:T(8,128)(2,1)}) %reduce-scatter.3.cloned.1.call-update) | async-done | bytes 786448 | tf_op jit(solution)/shard_map/reduce_scatter | solution.py:135
  159.6 1.8 copy.77
  161.4 1.6 constant_dynamic-slice_fusion
  163.1 1.5 collective-permute-start
  164.6 2.4 %collective-permute-start.1 = (bf16[1,96,1024]{2,0,1:T(2,128)(2,1)S(1)}, bf16[1,96,1024]{2,0,1:T(2,128)(2,1)S(1)}, u32[]{:S(2)}, u32[]{:S(2)}) collective-permute-start(bf16[1,96,1024]{2,0,1:T(2,128)(2,1)S(1)} %get-tuple-element.8), channel_id=1, source_target_pairs={{0,8},{4,12},{8,0},{12,4},{1,9},{5,13},{9,1},{13,5},{2,10},{6,14},... | collective-permute-start | bytes 589832 | tf_op jit(solution)/shard_map/ppermute | solution.py:22
  167.0 0.5 collective-permute-start.2
  167.7 13.7 %collective-permute-done = bf16[1,96,1024]{2,0,1:T(2,128)(2,1)S(1)} collective-permute-done((bf16[1,96,1024]{2,0,1:T(2,128)(2,1)S(1)}, bf16[1,96,1024]{2,0,1:T(2,128)(2,1)S(1)}, u32[]{:S(2)}, u32[]{:S(2)}) %collective-permute-start) | collective-permute-done | bytes 196640 | tf_op jit(solution)/shard_map/ppermute | solution.py:22
  181.4 12.9 %collective-permute-done.1 = bf16[1,96,1024]{2,0,1:T(2,128)(2,1)S(1)} collective-permute-done((bf16[1,96,1024]{2,0,1:T(2,128)(2,1)S(1)}, bf16[1,96,1024]{2,0,1:T(2,128)(2,1)S(1)}, u32[]{:S(2)}, u32[]{:S(2)}) %collective-permute-start.1) | collective-permute-done | bytes 196640 | tf_op jit(solution)/shard_map/ppermute | solution.py:22
  194.5 1.4 bitcast_convert_fusion
  195.9 5.1 %gather_fusion = f32[512,1024]{1,0:T(8,128)} fusion(f32[384,1024]{1,0:T(8,128)} %bitcast_convert_fusion, s32[1024]{0:T(1024)S(1)} %pad_clamp_fusion), kind=kCustom, calls=%fused_computation | custom fusion | bytes 4196352 | tf_op jit(solution)/shard_map/jit(_take)/gather | solution.py:63
  201.0 3.0 %fusion.15 = bf16[64,1024]{1,0:T(8,128)(2,1)} fusion(f32[512,1024]{1,0:T(8,128)} %gather_fusion, f32[64,8]{1,0:T(8,128)S(1)} %copy.83, pred[64,8]{1,0:T(8,128)(4,1)S(1)} %copy.72), kind=kLoop, calls=%fused_computation.14 | loop fusion | flops 1507328 | bytes 2230784 | tf_op jit(solution)/shard_map/reduce_sum | solution.py:67
  204.0 12.7 %reduce-scatter.5.cloned.1.call-done = bf16[64,512]{1,0:T(8,128)(2,1)} async-done(((bf16[64,1024]{1,0:T(8,128)(2,1)}), bf16[64,512]{1,0:T(8,128)(2,1)}) %reduce-scatter.5.cloned.1.call-update) | async-done | bytes 65552 | tf_op jit(solution)/shard_map/reduce_scatter | solution.py:145
  216.7 1.5 add_convert_fusion
  (36 shorter events, 0.8 us)
Async XLA Ops:
  6.5 12.4 %copy-start = (bf16[1024,1024]{1,0:T(8,128)(2,1)S(1)}, bf16[1024,1024]{1,0:T(8,128)(2,1)}, u32[]{:S(2)}) copy-start(bf16[1024,1024]{1,0:T(8,128)(2,1)} %param.20) | copy-start | bytes 6291460
  6.5 33.5 %all-reduce.2.cloned.1.call-start = ((), (), s32[]{:S(2)}) async-start(), calls=%async_computation.3 | async-start | bytes 262144 | tf_op jit(solution)/shard_map/psum | solution.py:92
  10.6 9.5 %copy-start.3 = (s32[64,8]{0,1:T(8,128)S(1)}, s32[64,8]{0,1:T(8,128)}, u32[]{:S(2)}) copy-start(s32[64,8]{0,1:T(8,128)} %param.23) | copy-start | bytes 6148
  12.9 27.1 %copy-start.2 = (bf16[64,1024]{1,0:T(8,128)(2,1)S(1)}, bf16[64,1024]{1,0:T(8,128)(2,1)}, u32[]{:S(2)}) copy-start(bf16[64,1024]{1,0:T(8,128)(2,1)} %param.21) | copy-start | bytes 393220
  13.0 33.0 %copy-start.5 = (f32[1024]{0:T(1024)S(1)}, f32[1024]{0:T(1024)}, u32[]{:S(2)}) copy-start(f32[1024]{0:T(1024)} %param.22) | copy-start | bytes 12292
  20.1 139.5 %reduce-scatter.3.cloned.1.call-start = ((), (), s32[]{:S(2)}) async-start(), calls=%async_computation.4 | async-start | bytes 3145728 | tf_op jit(solution)/shard_map/reduce_scatter | solution.py:135
  100.2 1.1 copy-start.1
  128.5 0.7 copy-start.4
  128.5 88.2 %reduce-scatter.5.cloned.1.call-start = ((), (), s32[]{:S(2)}) async-start(), calls=%async_computation.5 | async-start | bytes 196608 | tf_op jit(solution)/shard_map/reduce_scatter | solution.py:145
  163.1 18.3 %collective-permute-start = (bf16[1,96,1024]{2,0,1:T(2,128)(2,1)S(1)}, bf16[1,96,1024]{2,0,1:T(2,128)(2,1)S(1)}, u32[]{:S(2)}, u32[]{:S(2)}) collective-permute-start(bf16[1,96,1024]{2,0,1:T(2,128)(2,1)S(1)} %get-tuple-element.9), channel_id=1, source_target_pairs={{0,4},{4,0},{8,12},{12,8},{1,5},{5,1},{9,13},{13,9},{2,6},{6,2},{1... | collective-permute-start | bytes 589832 | tf_op jit(solution)/shard_map/ppermute | solution.py:22
  164.6 29.7 %collective-permute-start.1 = (bf16[1,96,1024]{2,0,1:T(2,128)(2,1)S(1)}, bf16[1,96,1024]{2,0,1:T(2,128)(2,1)S(1)}, u32[]{:S(2)}, u32[]{:S(2)}) collective-permute-start(bf16[1,96,1024]{2,0,1:T(2,128)(2,1)S(1)} %get-tuple-element.8), channel_id=1, source_target_pairs={{0,8},{4,12},{8,0},{12,4},{1,9},{5,13},{9,1},{13,5},{2,10},{6,14},... | collective-permute-start | bytes 589832 | tf_op jit(solution)/shard_map/ppermute | solution.py:22
  167.0 27.4 %collective-permute-start.2 = (bf16[1,96,1024]{2,0,1:T(2,128)(2,1)S(1)}, bf16[1,96,1024]{2,0,1:T(2,128)(2,1)S(1)}, u32[]{:S(2)}, u32[]{:S(2)}) collective-permute-start(bf16[1,96,1024]{2,0,1:T(2,128)(2,1)S(1)} %get-tuple-element.7), channel_id=1, source_target_pairs={{0,12},{4,8},{8,4},{12,0},{1,13},{5,9},{9,5},{13,1},{2,14},{6,10},... | collective-permute-start | bytes 589832 | tf_op jit(solution)/shard_map/ppermute | solution.py:22
Sparse Core Ops, SparseCore 0:
  20.2 19.6 all-reduce.1
  128.6 30.9 reduce-scatter.2
  204.1 12.5 reduce-scatter.4
